TPU v7x, 32 devices: a whole 2x2x4 slice. The times are simulated.
32 devices in a mesh: dp: 8 (over z, x), tensor: 4 (over y, core).
Axes of the slice: x: 2, y: 2, z: 4, core: 2. Of those that a mesh axis runs over, the one named last changes fastest.
Arguments:
- tokens: bfloat16 [16384, 768], P(('dp', 'tensor')), may hold values from -6 to 6
- segments: int32 [8, 2048], P('dp'), may hold values from 0 to 7, never falling along the last dimension, each value on 1 to 1024 neighbouring positions
- block_perm: int32 [12], P('tensor'), may hold values from 0 to 1
- w_qkv: bfloat16 [3, 768, 768], P(None, None, 'tensor'), may hold values from -0.21875 to 0.21875
- b_qv: bfloat16 [2, 768], P(None, 'tensor'), may hold values from -3 to 3
- w_out: bfloat16 [768, 768], P('tensor'), may hold values from -2.5 to 2.5
- b_out: bfloat16 [768], replicated, may hold values from -3 to 3
- ln1_gain: bfloat16 [768], replicated, may hold values from 0.5 to 1.5
- ln1_bias: bfloat16 [768], replicated, may hold values from -3 to 3
- w_up: bfloat16 [768, 3072], P(None, 'tensor'), may hold values from -0.21875 to 0.21875
- b_up: bfloat16 [3072], P('tensor'), may hold values from -3 to 3
- w_down: bfloat16 [3072, 768], P('tensor'), may hold values from -0.109375 to 0.109375
- b_down: bfloat16 [768], replicated, may hold values from -3 to 3
- ln2_gain: bfloat16 [768], replicated, may hold values from 0.5 to 1.5
- ln2_bias: bfloat16 [768], replicated, may hold values from -3 to 3
- cotangent: bfloat16 [16384, 768], P(('dp', 'tensor')), may hold values from -6 to 6
Outputs:
- out: bfloat16 [16384, 768], P(('dp', 'tensor'))
- grad_tokens: bfloat16 [16384, 768], P(('dp', 'tensor'))
- grad_w_qkv: float32 [3, 768, 768], P(None, None, 'tensor')
- grad_b_qv: float32 [2, 768], P(None, 'tensor')
- grad_w_out: float32 [768, 768], P('tensor')
- grad_b_out: float32 [768], replicated
- grad_ln1_gain: float32 [768], replicated
- grad_ln1_bias: float32 [768], replicated
- grad_w_up: float32 [768, 3072], P(None, 'tensor')
- grad_b_up: float32 [3072], P('tensor')
- grad_w_down: float32 [3072, 768], P('tensor')
- grad_b_down: float32 [768], replicated
- grad_ln2_gain: float32 [768], replicated
- grad_ln2_bias: float32 [768], replicated
Inputs may be any that keep to these rules, and one draw needn't show every extreme that they name: `segments`: within a sequence segment numbers never fall; each sequence holds 8 documents, the longest of half of 2048 tokens.
All inputs are finite; a program needn't handle non-finite values.
Results may differ from a plain program's by a relative error of at most 0.014.
Values may be sent and summed in bfloat16 or wider, within the bound.
No kernel may reach another device: no remote copies, remote signals or barrier semaphores. Data moves between devices by JAX's collectives and lax.ppermute only.
A program may use at most 128 MiB of HBM per device.

v0:
```python
import jax
import jax.numpy as jnp
from jax import lax
from jax.sharding import PartitionSpec as P

HEAD_SIZE = 64


epsilon = 1e-05


def norm_layer(resid, gain_vec, shift_vec):
    row_mean = jnp.mean(resid, axis=-1, keepdims=True)
    centered = resid - row_mean
    row_var = jnp.mean(centered * centered, axis=-1, keepdims=True)
    return centered * lax.rsqrt(row_var + epsilon) * gain_vec + shift_vec


def gelu_exact(pre_act):
    return jax.nn.gelu(pre_act, approximate=False)


def blocks_of(matrix, heads_local):
    seq_len = matrix.shape[0]
    head_dim = matrix.shape[1] // heads_local
    return (
        matrix.reshape(seq_len, heads_local, head_dim)
        .transpose(1, 0, 2)
        .reshape(heads_local * 2, seq_len // 2, head_dim)
    )


def rows_of(blocks, heads_local):
    half_len = blocks.shape[1]
    head_dim = blocks.shape[2]
    return (
        blocks.reshape(heads_local, half_len * 2, head_dim)
        .transpose(1, 0, 2)
        .reshape(half_len * 2, heads_local * head_dim)
    )


def swap_blocks(blocks, block_perm):
    heads_local = block_perm.shape[0]
    shaped = blocks.reshape((heads_local, 2) + blocks.shape[1:])
    flag_mask = (block_perm == 1).reshape((heads_local,) + (1,) * blocks.ndim)
    return jnp.where(flag_mask, shaped[:, ::-1], shaped).reshape(blocks.shape)


def block_scores(query_blk, key_blk, seg_query, seg_key):
    allowed = seg_query[:, None] == seg_key[None, :]
    score_matrix = jnp.einsum(
        "qd,kd->qk", query_blk, key_blk, preferred_element_type=jnp.float32
    ) * HEAD_SIZE ** (-0.5)
    raised_base = jnp.where(allowed, score_matrix, 0.0)
    return (allowed, score_matrix, raised_base)


def attend_block(packed):
    query_blk, key_blk, value_blk, seg_query, seg_key = packed
    allowed, score_matrix, raised_base = block_scores(query_blk, key_blk, seg_query, seg_key)
    row_max = jnp.maximum(jnp.max(jnp.where(allowed, score_matrix, -1e30), axis=1), 0.0)
    raised = jnp.where(allowed, jnp.exp(raised_base - row_max[:, None]), 0.0)
    denominator = jnp.exp(-row_max) + jnp.sum(raised, axis=1)
    attention_probability = raised / denominator[:, None]
    context_output = jnp.dot(
        attention_probability.astype(jnp.bfloat16), value_blk, preferred_element_type=jnp.float32
    )
    return (context_output.astype(jnp.bfloat16), row_max, denominator)


def attend_back(packed):
    query_blk, key_blk, value_blk, seg_query, seg_key, row_max, denominator, grad_ctx = packed
    allowed, score_matrix, raised_base = block_scores(query_blk, key_blk, seg_query, seg_key)
    raised = jnp.where(allowed, jnp.exp(raised_base - row_max[:, None]), 0.0)
    attention_probability = raised / denominator[:, None]
    grad_prob = jnp.einsum("qd,kd->qk", grad_ctx, value_blk, preferred_element_type=jnp.float32)
    delta_rows = jnp.sum(attention_probability * grad_prob, axis=1)
    grad_scores = (attention_probability * (grad_prob - delta_rows[:, None])).astype(jnp.bfloat16)
    scale_factor = HEAD_SIZE ** (-0.5)
    grad_query = jnp.dot(grad_scores, key_blk, preferred_element_type=jnp.float32) * scale_factor
    grad_key = (
        jnp.einsum("qk,qd->kd", grad_scores, query_blk, preferred_element_type=jnp.float32)
        * scale_factor
    )
    grad_value = jnp.einsum(
        "qk,qd->kd",
        attention_probability.astype(jnp.bfloat16),
        grad_ctx,
        preferred_element_type=jnp.float32,
    )
    return (grad_query, grad_key, grad_value)


def body(
    tokens,
    segments,
    block_perm,
    w_qkv,
    b_qv,
    w_out,
    b_out,
    ln1_gain,
    ln1_bias,
    w_up,
    b_up,
    w_down,
    b_down,
    ln2_gain,
    ln2_bias,
    cotangent,
):
    heads_local = block_perm.shape[0]
    width = tokens.shape[1]
    tensor_count = lax.axis_size("tensor")
    gathered = lax.all_gather(tokens, "tensor", axis=0, tiled=True)
    seq_len = gathered.shape[0]
    projected = jnp.einsum("sd,cde->cse", gathered, w_qkv, preferred_element_type=jnp.float32)
    bias_qv = b_qv.astype(jnp.float32)
    queries = (projected[0] + bias_qv[0]).astype(jnp.bfloat16)
    key_rows = projected[1].astype(jnp.bfloat16)
    values = (projected[2] + bias_qv[1]).astype(jnp.bfloat16)
    query_block_rows = blocks_of(queries, heads_local)
    key_block_rows = swap_blocks(blocks_of(key_rows, heads_local), block_perm)
    value_block_rows = swap_blocks(blocks_of(values, heads_local), block_perm)
    seg_query = jnp.tile(segments[0].reshape(2, seq_len // 2), (heads_local, 1))
    seg_key = swap_blocks(seg_query, block_perm)
    context_output, row_max, denominator = lax.map(
        attend_block, (query_block_rows, key_block_rows, value_block_rows, seg_query, seg_key)
    )
    context_rows = rows_of(context_output, heads_local)
    attended = lax.psum_scatter(
        jnp.dot(context_rows, w_out, preferred_element_type=jnp.float32),
        "tensor",
        scatter_dimension=0,
        tiled=True,
    )
    resid_one = tokens.astype(jnp.float32) + (attended + b_out.astype(jnp.float32))
    normed_one, ln1_pull = jax.vjp(
        norm_layer, resid_one, ln1_gain.astype(jnp.float32), ln1_bias.astype(jnp.float32)
    )
    hidden_in = lax.all_gather(normed_one.astype(jnp.bfloat16), "tensor", axis=0, tiled=True)
    pre_act = jnp.dot(hidden_in, w_up, preferred_element_type=jnp.float32) + b_up.astype(
        jnp.float32
    )
    activated, gelu_pull = jax.vjp(gelu_exact, pre_act)
    act_low = activated.astype(jnp.bfloat16)
    ffn_out = lax.psum_scatter(
        jnp.dot(act_low, w_down, preferred_element_type=jnp.float32),
        "tensor",
        scatter_dimension=0,
        tiled=True,
    ) + b_down.astype(jnp.float32)
    resid_two = normed_one + ffn_out
    output, ln2_pull = jax.vjp(
        norm_layer, resid_two, ln2_gain.astype(jnp.float32), ln2_bias.astype(jnp.float32)
    )
    grad_resid_two, grad_ln2_gain, grad_ln2_bias = ln2_pull(cotangent.astype(jnp.float32))
    grad_ffn_rows = lax.all_gather(
        grad_resid_two.astype(jnp.bfloat16), "tensor", axis=0, tiled=True
    )
    grad_b_down = jnp.sum(grad_ffn_rows, axis=0, dtype=jnp.float32)
    grad_w_down = jnp.einsum(
        "sf,sd->fd", act_low, grad_ffn_rows, preferred_element_type=jnp.float32
    )
    grad_act = jnp.einsum("sd,fd->sf", grad_ffn_rows, w_down, preferred_element_type=jnp.float32)
    (grad_pre,) = gelu_pull(grad_act)
    grad_pre_low = grad_pre.astype(jnp.bfloat16)
    grad_b_up = jnp.sum(grad_pre_low, axis=0, dtype=jnp.float32)
    grad_w_up = jnp.einsum("sd,sf->df", hidden_in, grad_pre_low, preferred_element_type=jnp.float32)
    grad_normed = grad_resid_two + lax.psum_scatter(
        jnp.einsum("sf,df->sd", grad_pre_low, w_up, preferred_element_type=jnp.float32),
        "tensor",
        scatter_dimension=0,
        tiled=True,
    )
    grad_resid_one, grad_ln1_gain, grad_ln1_bias = ln1_pull(grad_normed)
    grad_attn_rows = lax.all_gather(
        grad_resid_one.astype(jnp.bfloat16), "tensor", axis=0, tiled=True
    )
    grad_b_out = jnp.sum(grad_attn_rows, axis=0, dtype=jnp.float32)
    grad_w_out = jnp.einsum(
        "se,sd->ed", context_rows, grad_attn_rows, preferred_element_type=jnp.float32
    )
    grad_context = jnp.einsum(
        "sd,ed->se", grad_attn_rows, w_out, preferred_element_type=jnp.float32
    ).astype(jnp.bfloat16)
    grad_ctx_blocks = blocks_of(grad_context, heads_local)
    grad_query, grad_key, grad_value = lax.map(
        attend_back,
        (
            query_block_rows,
            key_block_rows,
            value_block_rows,
            seg_query,
            seg_key,
            row_max,
            denominator,
            grad_ctx_blocks,
        ),
    )
    grad_key = swap_blocks(grad_key, block_perm)
    grad_value = swap_blocks(grad_value, block_perm)
    grad_proj = jnp.stack(
        [
            rows_of(grad_query, heads_local),
            rows_of(grad_key, heads_local),
            rows_of(grad_value, heads_local),
        ]
    ).astype(jnp.bfloat16)
    grad_b_qv = jnp.stack(
        [
            jnp.sum(grad_proj[0], axis=0, dtype=jnp.float32),
            jnp.sum(grad_proj[2], axis=0, dtype=jnp.float32),
        ]
    )
    grad_w_qkv = jnp.einsum("sd,cse->cde", gathered, grad_proj, preferred_element_type=jnp.float32)
    grad_in_part = jnp.einsum("cse,cde->sd", grad_proj, w_qkv, preferred_element_type=jnp.float32)
    norm_grads = jnp.stack([grad_ln1_gain, grad_ln1_bias, grad_ln2_gain, grad_ln2_bias])
    norm_tiled = jnp.broadcast_to(norm_grads[None], (tensor_count, 4, width))
    grad_in_local, norm_summed = (
        lax.psum_scatter(grad_in_part, "tensor", scatter_dimension=0, tiled=True),
        lax.psum_scatter(norm_tiled, "tensor", scatter_dimension=0, tiled=True),
    )
    grad_tokens = (grad_resid_one + grad_in_local).astype(jnp.bfloat16)
    norm_summed = norm_summed[0]
    (
        grad_w_qkv,
        grad_b_qv,
        grad_w_out,
        grad_b_out,
        norm_summed,
        grad_w_up,
        grad_b_up,
        grad_w_down,
        grad_b_down,
    ) = lax.psum(
        (
            grad_w_qkv,
            grad_b_qv,
            grad_w_out,
            grad_b_out,
            norm_summed,
            grad_w_up,
            grad_b_up,
            grad_w_down,
            grad_b_down,
        ),
        "dp",
    )
    return (
        output.astype(jnp.bfloat16),
        grad_tokens,
        grad_w_qkv,
        grad_b_qv,
        grad_w_out,
        grad_b_out,
        norm_summed[0],
        norm_summed[1],
        grad_w_up,
        grad_b_up,
        grad_w_down,
        grad_b_down,
        norm_summed[2],
        norm_summed[3],
    )


def solution(mesh):
    placed = (
        P(("dp", "tensor"), None),
        P("dp", None),
        P("tensor"),
        P(None, None, "tensor"),
        P(None, "tensor"),
        P("tensor", None),
        P(),
        P(),
        P(),
        P(None, "tensor"),
        P("tensor"),
        P("tensor", None),
        P(),
        P(),
        P(),
        P(("dp", "tensor"), None),
    )
    return jax.shard_map(
        body,
        mesh=mesh,
        in_specs=placed,
        out_specs=(
            P(("dp", "tensor"), None),
            P(("dp", "tensor"), None),
            P(None, None, "tensor"),
            P(None, "tensor"),
            P("tensor", None),
            P(),
            P(),
            P(),
            P(None, "tensor"),
            P("tensor"),
            P("tensor", None),
            P(),
            P(),
            P(),
        ),
        check_vma=False,
    )
```

profile of v0, /device:TPU:0, one launch (start us, length us, event | category | flops | bytes accessed | tf_op | source)
XLA Modules:
  0.0 848.9 jit_solution(5124570550672903367)
XLA Ops:
  13.0 27.8 %all-gather.5.cloned.1.call-done = bf16[2048,768]{1,0:T(8,128)(2,1)} async-done(((bf16[512,768]{1,0:T(8,128)(2,1)}), bf16[2048,768]{1,0:T(8,128)(2,1)}) %all-gather.5.cloned.1.call-update) | async-done | bytes 3145744 | tf_op jit(solution)/shard_map/all_gather | solution.py:116
  40.8 4.2 convolution_bitcast_fusion.1
  49.8 2.5 copy.57
  52.2 59.4 %while.28 = (s32[]{:T(128)}, bf16[6,1024,64]{1,2,0:T(8,128)(2,1)}, f32[6,1024]{1,0:T(8,128)}, f32[6,1024]{1,0:T(8,128)}, s32[6,1024]{1,0:T(8,128)}, /*index=5*/s...) while((s32[]{:T(128)}, bf16[6,1024,64]{1,2,0:T(8,128)(2,1)}, ...), condition=%wide.region_3.4_spmd, body=%wide.region_0.3_spmd.sunk | while | flops 286330880 | bytes 13613185 | solution.py:128
  53.0 1.7 fusion.131
  56.3 3.1 fusion.133
  62.9 1.7 fusion.131
  66.2 3.1 fusion.133
  72.8 1.7 fusion.131
  76.1 3.1 fusion.133
  82.7 1.7 fusion.131
  86.0 3.1 fusion.133
  92.6 1.7 fusion.131
  95.9 3.1 fusion.133
  102.5 1.7 fusion.131
  105.8 3.1 fusion.133
  111.6 3.2 copy.61
  114.8 3.6 reshape.217
  118.4 1.8 copy.62
  121.1 3.7 fusion.86
  125.6 58.3 %reduce-scatter.5.cloned.1.call-done = f32[512,768]{1,0:T(8,128)} async-done(((f32[2048,768]{1,0:T(8,128)}), f32[512,768]{1,0:T(8,128)}) %reduce-scatter.5.cloned.1.call-update) | async-done | bytes 1572880 | tf_op jit(solution)/shard_map/reduce_scatter | solution.py:132
  183.9 1.7 fusion.84
  187.4 28.4 %all-gather.7.cloned.1.call-done = bf16[2048,768]{1,0:T(8,128)(2,1)} async-done(((bf16[512,768]{1,0:T(8,128)(2,1)}), bf16[2048,768]{1,0:T(8,128)(2,1)}) %all-gather.7.cloned.1.call-update) | async-done | bytes 3145744 | tf_op jit(solution)/shard_map/all_gather | solution.py:142
  215.8 18.4 %multiply_convert_fusion.1 = (bf16[2048,768]{1,0:T(8,128)(2,1)S(1)}, f32[2048,768]{1,0:T(8,128)}, f32[2048,768]{1,0:T(8,128)}) fusion(f32[768]{0:T(1024)S(1)} %convert_element_type.106, bf16[2048,768]{1,0:T(8,128)(2,1)} %all-gather.7.cloned.1.call-done, bf16[768,768]{1,0:T(8,128)(2,1)S(1)} %copy-done), kind=kOutput, calls=%fused_computation.75 | convolution fusion | flops 2519728128 | bytes 20057088 | tf_op jit(solution)/shard_map/dot_general | solution.py:143
  234.3 1.8 copy-done.40
  236.0 4.5 fusion.87
  242.4 57.1 %reduce-scatter.7.cloned.1.call-done = f32[512,768]{1,0:T(8,128)} async-done(((f32[2048,768]{1,0:T(8,128)}), f32[512,768]{1,0:T(8,128)}) %reduce-scatter.7.cloned.1.call-update) | async-done | bytes 1572880 | tf_op jit(solution)/shard_map/reduce_scatter | solution.py:148
  299.5 2.0 fusion.82
  307.1 28.4 %all-gather.9.cloned.1.call-done = bf16[2048,768]{1,0:T(8,128)(2,1)} async-done(((bf16[512,768]{1,0:T(8,128)(2,1)}), bf16[2048,768]{1,0:T(8,128)(2,1)}) %all-gather.9.cloned.1.call-update) | async-done | bytes 3145744 | tf_op jit(solution)/shard_map/all_gather | solution.py:159
  335.5 10.5 %convert_reduce_fusion.1 = (f32[768]{0:T(1024)S(1)}, bf16[2048,768]{1,0:T(8,128)(2,1)S(1)}) fusion(f32[2048,768]{1,0:T(8,128)} %get-tuple-element.206, f32[2048,768]{1,0:T(8,128)} %get-tuple-element.226, f32[768]{0:T(1024)S(1)} %copy-done.28, bf16[2048,768]{1,0:T(8,128)(2,1)} %all-gather.9.cloned.1.call-done, bf16[768,768]{1,0:T(8,128)(2,1)} %param.31), kind=kOutput, calls=%fused_computation.72 | convolution fusion | flops 2442657024 | bytes 20060160 | tf_op jit(solution)/shard_map/sd,fd->sf/dot_general | solution.py:166
  346.0 1.7 copy-done.41
  347.7 4.5 fusion.88
  352.3 58.9 %reduce-scatter.9.cloned.1.call-done = f32[512,768]{1,0:T(8,128)} async-done(((f32[2048,768]{1,0:T(8,128)}), f32[512,768]{1,0:T(8,128)}) %reduce-scatter.9.cloned.1.call-update) | async-done | bytes 1572880 | tf_op jit(solution)/shard_map/reduce_scatter | solution.py:171
  411.3 2.7 multiply_reduce_fusion.1
  417.2 28.3 %all-gather.11.cloned.1.call-done = bf16[2048,768]{1,0:T(8,128)(2,1)} async-done(((bf16[512,768]{1,0:T(8,128)(2,1)}), bf16[2048,768]{1,0:T(8,128)(2,1)}) %all-gather.11.cloned.1.call-update) | async-done | bytes 3145744 | tf_op jit(solution)/shard_map/all_gather | solution.py:178
  445.6 3.1 convolution_convert_fusion
  449.5 75.2 %while.29 = (s32[]{:T(128)}, bf16[6,1024,64]{1,2,0:T(8,128)(2,1)S(1)}, bf16[6,1024,64]{1,2,0:T(8,128)(2,1)}, bf16[6,1024,64]{1,2,0:T(8,128)(2,1)}, s32[6,1024]{1...) while((s32[]{:T(128)}, ...), condition=%wide.region_17.18_spmd, body=%wide.region_15.17_spmd.sunk | while | flops 683801600 | bytes 34141324 | solution.py:189
  452.8 2.8 multiply_reduce_fusion.6
  458.2 2.4 fusion.144
  465.3 2.8 multiply_reduce_fusion.6
  470.7 2.4 fusion.144
  476.2 1.7 fusion.142
  477.8 2.8 multiply_reduce_fusion.6
  483.2 2.4 fusion.144
  490.4 2.8 multiply_reduce_fusion.6
  495.8 2.4 fusion.144
  501.2 1.7 fusion.142
  502.9 2.8 multiply_reduce_fusion.6
  508.3 2.4 fusion.144
  513.8 1.7 fusion.142
  515.5 2.8 multiply_reduce_fusion.6
  520.9 2.4 fusion.144
  524.8 2.7 fusion.75
  531.2 7.0 convolution_bitcast_fusion
  538.6 7.1 fusion.91
  545.7 4.2 fusion.90
  551.7 3.2 fusion.69
  556.2 2.4 convert_reduce_fusion
  558.7 13.2 %all-reduce = f32[4,4,768]{2,1,0:T(4,128)S(1)} all-reduce(f32[4,4,768]{2,1,0:T(4,128)S(1)} %broadcast_in_dim.105), channel_id=6, replica_groups=mesh['dp'=8,'tensor'=4] {'tensor'}, use_global_device_ids=true, to_apply=%region_30.31.clone | all-reduce | flops 12288 | bytes 98304
  573.0 2.4 convert_reduce_fusion.2
  575.4 37.9 %all-reduce.1 = (f32[2,192]{1,0:T(2,128)}, f32[768]{0:T(1024)}, f32[4,768]{1,0:T(4,128)S(1)}, f32[768]{0:T(1024)}, f32[768]{0:T(1024)}) all-reduce(f32[2,192]{1,0:T(2,128)S(1)} %pad_maximum_fusion.4, f32[768]{0:T(1024)S(1)} %convert_reduce_fusion.2, ...), channel_id=1, replica_groups=mesh['dp'=8,'tensor'=4] {'dp'}, use_global_device_ids=true, to_apply=%region_22.23 | all-reduce | flops 5760 | bytes 46080 | tf_op jit(solution)/shard_map/psum | solution.py:237
  613.9 2.5 add_convert_fusion.1
  616.4 218.8 %all-reduce.5.cloned.1.call-done = (f32[3,768,192]{1,2,0:T(8,128)}, f32[192,768]{1,0:T(8,128)}, f32[768,768]{1,0:T(8,128)}, f32[768,768]{1,0:T(8,128)}) async-done(((f32[3,768,192]{1,2,0:T(8,128)}, f32[192,768]{1,0:T(8,128)}, f32[768,768]{1,0:T(8,128)}, f32[768,768]{1,0:T(8,128)}), (f32[3,768,192]{1,2,0:T(8,128)}, f32[192,768]{1,0:T(8,128)}, f32[768,768]{1,0:T(8,128)}, ...) | async-done | bytes 7077904 | tf_op jit(solution)/shard_map/psum | solution.py:237
  835.2 2.9 copy.110
  (250 shorter events, 107.5 us)
Async XLA Ops:
  7.2 208.6 %copy-start = (bf16[768,768]{1,0:T(8,128)(2,1)S(1)}, bf16[768,768]{1,0:T(8,128)(2,1)}, u32[]{:S(2)}) copy-start(bf16[768,768]{1,0:T(8,128)(2,1)} %param.29) | copy-start | bytes 3538948
  7.2 33.6 %all-gather.5.cloned.1.call-start = ((), (), s32[]{:S(2)}) async-start(), calls=%async_computation.4 | async-start | bytes 3932160 | tf_op jit(solution)/shard_map/all_gather | solution.py:116
  7.9 176.0 %reduce-scatter.5.cloned.1.call-start = ((), (), s32[]{:S(2)}) async-start(), calls=%async_computation.5 | async-start | bytes 7864320 | tf_op jit(solution)/shard_map/reduce_scatter | solution.py:132
  12.3 33.4 %copy-start.25 = (pred[3]{0:T(512)(128)(4,1)}, pred[3]{0:T(512)(128)(4,1)S(1)}, u32[]{:S(2)}) copy-start(pred[3]{0:T(512)(128)(4,1)S(1)} %broadcast_compare_fusion) | copy-start | bytes 13
  111.6 13.2 %copy-start.8 = (bf16[6,1024,64]{2,1,0:T(8,128)(2,1)}, bf16[6,1024,64]{2,1,0:T(8,128)(2,1)S(1)}, u32[]{:S(2)}) copy-start(bf16[6,1024,64]{2,1,0:T(8,128)(2,1)S(1)} %get-tuple-element.489) | copy-start | bytes 2359300
  111.6 9.5 %copy-start.17 = (bf16[192,768]{1,0:T(8,128)(2,1)S(1)}, bf16[192,768]{1,0:T(8,128)(2,1)}, u32[]{:S(2)}) copy-start(bf16[192,768]{1,0:T(8,128)(2,1)} %param.25) | copy-start | bytes 884740
  120.2 0.9 copy-start.6
  124.8 0.7 copy-start.29
  124.8 0.7 copy-start.30
  124.8 0.7 copy-start.31
  124.9 59.0 %copy-start.12 = (bf16[512,768]{1,0:T(8,128)(2,1)S(1)}, bf16[512,768]{1,0:T(8,128)(2,1)}, u32[]{:S(2)}) copy-start(bf16[512,768]{1,0:T(8,128)(2,1)} %param.20) | copy-start | bytes 2359300
  124.9 90.9 %all-gather.7.cloned.1.call-start = ((), (), s32[]{:S(2)}) async-start(), calls=%async_computation.6 | async-start | bytes 3932160 | tf_op jit(solution)/shard_map/all_gather | solution.py:142
  125.6 61.6 %copy-start.19 = (f32[768]{0:T(1024)}, f32[768]{0:T(1024)S(1)}, u32[]{:S(2)}) copy-start(f32[768]{0:T(1024)S(1)} %convert_element_type.104) | copy-start | bytes 9220
  185.6 1.8 copy-start.32
  185.9 48.4 %copy-start.20 = (f32[512]{0:T(512)}, f32[512]{0:T(512)S(1)}, u32[]{:S(2)}) copy-start(f32[512]{0:T(512)S(1)} %multiply_reduce_fusion.4) | copy-start | bytes 6148
  187.1 112.4 %reduce-scatter.7.cloned.1.call-start = ((), (), s32[]{:S(2)}) async-start(), calls=%async_computation.7 | async-start | bytes 7864320 | tf_op jit(solution)/shard_map/reduce_scatter | solution.py:148
  187.4 46.9 %copy-start.27 = (f32[768]{0:T(1024)}, f32[768]{0:T(1024)S(1)}, u32[]{:S(2)}) copy-start(f32[768]{0:T(1024)S(1)} %convert_element_type.106) | copy-start | bytes 9220
  215.8 20.2 %copy-start.38 = (bf16[768,768]{1,0:T(8,128)(2,1)S(1)}, bf16[768,768]{1,0:T(8,128)(2,1)}, u32[]{:S(2)}) copy-start(bf16[768,768]{1,0:T(8,128)(2,1)} %param.31) | copy-start | bytes 3538948
  234.2 1.8 copy-start.40
  240.5 0.7 copy-start.33
  240.5 0.7 copy-start.34
  240.5 1.3 copy-start.35
  240.5 95.0 %all-gather.9.cloned.1.call-start = ((), (), s32[]{:S(2)}) async-start(), calls=%async_computation.8 | async-start | bytes 3932160 | tf_op jit(solution)/shard_map/all_gather | solution.py:159
  242.4 59.4 %copy-start.9 = (bf16[512,768]{1,0:T(8,128)(2,1)S(1)}, bf16[512,768]{1,0:T(8,128)(2,1)}, u32[]{:S(2)}) copy-start(bf16[512,768]{1,0:T(8,128)(2,1)} %param.35) | copy-start | bytes 2359300
  301.5 1.6 copy-start.24
  304.7 1.1 copy-start.4
  304.7 30.9 %copy-start.28 = (f32[768]{0:T(1024)S(1)}, f32[768]{0:T(1024)}, u32[]{:S(2)}) copy-start(f32[768]{0:T(1024)} %copy-done.27) | copy-start | bytes 9220
  306.9 104.4 %reduce-scatter.9.cloned.1.call-start = ((), (), s32[]{:S(2)}) async-start(), calls=%async_computation.9 | async-start | bytes 7864320 | tf_op jit(solution)/shard_map/reduce_scatter | solution.py:171
  346.0 1.7 copy-start.41
  352.3 61.7 %copy-start.21 = (f32[512]{0:T(512)S(1)}, f32[512]{0:T(512)}, u32[]{:S(2)}) copy-start(f32[512]{0:T(512)} %copy-done.20) | copy-start | bytes 6148
  352.3 93.3 %all-gather.11.cloned.1.call-start = ((), (), s32[]{:S(2)}) async-start(), calls=%async_computation.10 | async-start | bytes 3932160 | tf_op jit(solution)/shard_map/all_gather | solution.py:178
  414.0 31.5 %copy-start.18 = (bf16[192,768]{1,0:T(8,128)(2,1)S(1)}, bf16[192,768]{1,0:T(8,128)(2,1)}, u32[]{:S(2)}) copy-start(bf16[192,768]{1,0:T(8,128)(2,1)} %param.25) | copy-start | bytes 884740
  414.7 1.1 copy-start.2
  416.9 197.0 %reduce-scatter.11.cloned.1.call-start = ((), (), s32[]{:S(2)}) async-start(), calls=%async_computation.11 | async-start | bytes 7864320 | tf_op jit(solution)/shard_map/reduce_scatter | solution.py:222
  449.5 75.3 %copy-start.26 = (pred[3]{0:T(512)(128)(4,1)S(1)}, pred[3]{0:T(512)(128)(4,1)}, u32[]{:S(2)}) copy-start(pred[3]{0:T(512)(128)(4,1)} %copy-done.25) | copy-start | bytes 13
  538.2 297.0 %all-reduce.5.cloned.1.call-start = ((), (), s32[]{:S(2)}) async-start(), calls=%async_computation.12 | async-start | bytes 14155776 | tf_op jit(solution)/shard_map/psum | solution.py:237
  538.6 7.1 copy-start.37
  538.6 7.1 copy-start.42
  545.7 4.2 copy-start.5
  545.7 4.2 copy-start.7
  545.7 5.9 copy-start.36
  549.9 1.7 copy-start.10
  549.9 1.9 copy-start.15
  554.9 0.7 copy-start.39
  554.9 1.2 copy-start.23
  554.9 1.2 copy-start.22
  555.0 17.8 %copy-start.11 = (bf16[3,2,8,8,1024]{4,3,1,2,0:T(8,128)(2,1)S(1)}, bf16[3,2,8,8,1024]{4,3,1,2,0:T(8,128)(2,1)}, u32[]{:S(2)}) copy-start(bf16[3,2,8,8,1024]{4,3,1,2,0:T(8,128)(2,1)} %copy.71) | copy-start | bytes 2359300
  558.6 55.3 %copy-start.3 = (f32[512,768]{1,0:T(8,128)S(1)}, f32[512,768]{1,0:T(8,128)}, u32[]{:S(2)}) copy-start(f32[512,768]{1,0:T(8,128)} %copy-done.2) | copy-start | bytes 4718596
  835.2 3.0 copy-start.16
  835.2 3.8 copy-start.14
  838.2 2.2 copy-start.13
  839.0 2.8 copy-start.1
Sparse Core Ops, SparseCore 0:
  9.6 31.2 all-gather.4
  125.0 58.8 reduce-scatter.4
  187.3 28.4 all-gather.6
  240.6 58.8 reduce-scatter.6
  307.0 28.4 all-gather.8
  352.4 58.8 reduce-scatter.8
  417.0 28.4 all-gather.10
  538.4 59.6 reduce-scatter.10
  603.6 231.5 all-reduce.4
where the time goes:
time: 860 us; the launch traced here: 849 us
  waiting for transfers between devices  507 us (59%)
  matrix products  159 us (18%)
  local copies, waits for them, and re-layouts  68.9 us (8%)
  blocking collectives  51.2 us (6%)
  other arithmetic  46.2 us (5%)
  between operations  14.9 us (2%)
    psum x1, waiting for transfers between devices, body(): lax.psum((grad_w_qkv, grad_b_qv, grad_w_out, grad_b_out, norm_summed, gra...  219 us
    reduce_scatter x1, waiting for transfers between devices, body(): lax.psum_scatter(jnp.einsum('sf,df->sd', grad_pre_low, w_up, preferred_el...  58.9 us
    reduce_scatter x1, waiting for transfers between devices, body(): lax.psum_scatter(jnp.dot(context_rows, w_out, preferred_element_type=jnp....  58.3 us
    reduce_scatter x1, waiting for transfers between devices, body(): lax.psum_scatter(jnp.dot(act_low, w_down, preferred_element_type=jnp.floa...  57.1 us
    psum x1, blocking collectives, body(): lax.psum((grad_w_qkv, grad_b_qv, grad_w_out, grad_b_out, norm_summed, gra...  37.9 us
    all_gather x1, waiting for transfers between devices, body(): lax.all_gather(grad_resid_two.astype(jnp.bfloat16), 'tensor', axis=0, til...  28.4 us
    all_gather x1, waiting for transfers between devices, body(): lax.all_gather(normed_one.astype(jnp.bfloat16), 'tensor', axis=0, tiled=T...  28.4 us
    all_gather x1, waiting for transfers between devices, body(): lax.all_gather(grad_resid_one.astype(jnp.bfloat16), 'tensor', axis=0, til...  28.3 us
  transfers between devices with their start and end apart: 9, of which 8 were waited for; matrix products, arithmetic and copies ran while one was open for 4% of the time, Pallas kernels for 0%

commit v1 on v0

--- a/solution.py
+++ b/solution.py
@@ -130,7 +130,7 @@
     )
     context_rows = rows_of(context_output, heads_local)
     attended = lax.psum_scatter(
-        jnp.dot(context_rows, w_out, preferred_element_type=jnp.float32),
+        jnp.dot(context_rows, w_out, preferred_element_type=jnp.bfloat16),
         "tensor",
         scatter_dimension=0,
         tiled=True,
@@ -146,7 +146,7 @@
     activated, gelu_pull = jax.vjp(gelu_exact, pre_act)
     act_low = activated.astype(jnp.bfloat16)
     ffn_out = lax.psum_scatter(
-        jnp.dot(act_low, w_down, preferred_element_type=jnp.float32),
+        jnp.dot(act_low, w_down, preferred_element_type=jnp.bfloat16),
         "tensor",
         scatter_dimension=0,
         tiled=True,
@@ -169,7 +169,7 @@
     grad_b_up = jnp.sum(grad_pre_low, axis=0, dtype=jnp.float32)
     grad_w_up = jnp.einsum("sd,sf->df", hidden_in, grad_pre_low, preferred_element_type=jnp.float32)
     grad_normed = grad_resid_two + lax.psum_scatter(
-        jnp.einsum("sf,df->sd", grad_pre_low, w_up, preferred_element_type=jnp.float32),
+        jnp.einsum("sf,df->sd", grad_pre_low, w_up, preferred_element_type=jnp.bfloat16),
         "tensor",
         scatter_dimension=0,
         tiled=True,
@@ -215,7 +215,7 @@
         ]
     )
     grad_w_qkv = jnp.einsum("sd,cse->cde", gathered, grad_proj, preferred_element_type=jnp.float32)
-    grad_in_part = jnp.einsum("cse,cde->sd", grad_proj, w_qkv, preferred_element_type=jnp.float32)
+    grad_in_part = jnp.einsum("cse,cde->sd", grad_proj, w_qkv, preferred_element_type=jnp.bfloat16)
     norm_grads = jnp.stack([grad_ln1_gain, grad_ln1_bias, grad_ln2_gain, grad_ln2_bias])
     norm_tiled = jnp.broadcast_to(norm_grads[None], (tensor_count, 4, width))
     grad_in_local, norm_summed = (
@@ -224,29 +224,12 @@
     )
     grad_tokens = (grad_resid_one + grad_in_local).astype(jnp.bfloat16)
     norm_summed = norm_summed[0]
-    (
-        grad_w_qkv,
-        grad_b_qv,
-        grad_w_out,
-        grad_b_out,
-        norm_summed,
-        grad_w_up,
-        grad_b_up,
-        grad_w_down,
-        grad_b_down,
-    ) = lax.psum(
-        (
-            grad_w_qkv,
-            grad_b_qv,
-            grad_w_out,
-            grad_b_out,
-            norm_summed,
-            grad_w_up,
-            grad_b_up,
-            grad_w_down,
-            grad_b_down,
-        ),
-        "dp",
+    grad_w_qkv, grad_w_out, grad_w_up, grad_w_down = (
+        lax.psum(v.astype(jnp.bfloat16), "dp").astype(jnp.float32)
+        for v in (grad_w_qkv, grad_w_out, grad_w_up, grad_w_down)
+    )
+    (grad_b_qv, grad_b_out, norm_summed, grad_b_up, grad_b_down) = lax.psum(
+        (grad_b_qv, grad_b_out, norm_summed, grad_b_up, grad_b_down), "dp"
     )
     return (
         output.astype(jnp.bfloat16),

time: 860 us -> 692 us (0.80)
  waiting for transfers between devices: 507 us -> 319 us
  other arithmetic: 46.2 us -> 58.4 us
    psum x1, waiting for transfers between devices: 219 us -> 74.4 us  [body(): lax.psum(v.astype(jnp.bfloat16), 'dp').astype(jnp.float32)]
    reduce_scatter x1, waiting for transfers between devices: 0.01 us -> 32.7 us  [body(): lax.psum_scatter(grad_in_part, 'tensor', scatter_dimension=0, tiled=True)]
    reduce_scatter x1, waiting for transfers between devices: 57.1 us -> 34.1 us  [body(): lax.psum_scatter(jnp.dot(act_low, w_down, preferred_element_type=jnp.bflo...]
    reduce_scatter x1, waiting for transfers between devices: 58.3 us -> 37.3 us  [body(): lax.psum_scatter(jnp.dot(context_rows, w_out, preferred_element_type=jnp....]
    reduce_scatter x1, waiting for transfers between devices: 58.9 us -> 38 us  [body(): lax.psum_scatter(jnp.einsum('sf,df->sd', grad_pre_low, w_up, preferred_el...]
    while x0 -> x12, local copies, waits for them, and re-layouts: none -> 11.4 us
    all_gather x1, waiting for transfers between devices: 28.3 us -> 17.5 us  [body(): lax.all_gather(grad_resid_one.astype(jnp.bfloat16), 'tensor', axis=0, til...]
  transfers between devices with their start and end apart: 9 -> 9, of which waited for: 8 -> 9; matrix products, arithmetic and copies ran while one was open for 4% -> 6% of each run, Pallas kernels for 0% -> 0%
where the time goes in v1:
time: 692 us; the launch traced here: 680 us
  waiting for transfers between devices  319 us (46%)
  matrix products  162 us (23%)
  local copies, waits for them, and re-layouts  73 us (11%)
  other arithmetic  58.4 us (8%)
  blocking collectives  50.9 us (7%)
  between operations  14.6 us (2%)
    psum x1, waiting for transfers between devices, body(): lax.psum(v.astype(jnp.bfloat16), 'dp').astype(jnp.float32)  74.4 us
    psum x1, blocking collectives, body(): lax.psum((grad_b_qv, grad_b_out, norm_summed, grad_b_up, grad_b_down), 'dp')  39.2 us
    reduce_scatter x1, waiting for transfers between devices, body(): lax.psum_scatter(jnp.einsum('sf,df->sd', grad_pre_low, w_up, preferred_el...  38 us
    reduce_scatter x1, waiting for transfers between devices, body(): lax.psum_scatter(jnp.dot(context_rows, w_out, preferred_element_type=jnp....  37.3 us
    reduce_scatter x1, waiting for transfers between devices, body(): lax.psum_scatter(jnp.dot(act_low, w_down, preferred_element_type=jnp.bflo...  34.1 us
    reduce_scatter x1, waiting for transfers between devices, body(): lax.psum_scatter(grad_in_part, 'tensor', scatter_dimension=0, tiled=True)  32.7 us
    all_gather x1, waiting for transfers between devices, body(): lax.all_gather(grad_resid_two.astype(jnp.bfloat16), 'tensor', axis=0, til...  28.4 us
    all_gather x1, waiting for transfers between devices, body(): lax.all_gather(normed_one.astype(jnp.bfloat16), 'tensor', axis=0, tiled=T...  28.4 us
  transfers between devices with their start and end apart: 9, of which 9 were waited for; matrix products, arithmetic and copies ran while one was open for 6% of the time, Pallas kernels for 0%

profile of v1, /device:TPU:0, one launch (start us, length us, event | category | flops | bytes accessed | tf_op | source)
XLA Modules:
  0.0 680.3 jit_solution(709475917562655532)
XLA Ops:
  13.0 27.8 %all-gather.5.cloned.1.call-done = bf16[2048,768]{1,0:T(8,128)(2,1)} async-done(((bf16[512,768]{1,0:T(8,128)(2,1)}), bf16[2048,768]{1,0:T(8,128)(2,1)}) %all-gather.5.cloned.1.call-update) | async-done | bytes 3145744 | tf_op jit(solution)/shard_map/all_gather | solution.py:116
  40.8 4.2 convolution_bitcast_fusion
  47.2 2.4 copy.57
  52.2 78.2 %while.28 = (s32[]{:T(128)}, bf16[6,1024,64]{1,2,0:T(8,128)(2,1)}, f32[6,1024]{1,0:T(8,128)}, f32[6,1024]{1,0:T(8,128)}, s32[6,1024]{1,0:T(8,128)}, /*index=5*/s...) while((s32[]{:T(128)}, bf16[6,1024,64]{1,2,0:T(8,128)(2,1)}, ...), condition=%wide.region_3.4_spmd, body=%wide.region_0.3_spmd.sunk | while | flops 286330880 | bytes 30390420 | solution.py:128
  53.0 1.7 fusion.133
  54.7 1.9 copy-done.2
  59.6 4.3 fusion.135
  66.0 1.7 fusion.133
  67.8 1.9 copy-done.2
  72.6 4.3 fusion.135
  79.1 1.7 fusion.133
  80.8 1.9 copy-done.2
  85.6 4.3 fusion.135
  93.8 1.9 copy-done.2
  98.6 4.3 fusion.135
  106.8 1.9 copy-done.2
  111.7 4.3 fusion.135
  119.8 1.9 copy-done.2
  124.7 4.3 fusion.135
  130.4 3.2 copy.61
  133.5 3.6 reshape.217
  137.1 1.8 copy.62
  139.8 2.7 fusion.91
  143.3 37.3 %reduce-scatter.5.cloned.1.call-done = bf16[512,768]{1,0:T(8,128)(2,1)} async-done(((bf16[2048,768]{1,0:T(8,128)(2,1)}), bf16[512,768]{1,0:T(8,128)(2,1)}) %reduce-scatter.5.cloned.1.call-update) | async-done | bytes 786448 | tf_op jit(solution)/shard_map/reduce_scatter | solution.py:132
  185.4 28.4 %all-gather.7.cloned.1.call-done = bf16[2048,768]{1,0:T(8,128)(2,1)} async-done(((bf16[512,768]{1,0:T(8,128)(2,1)}), bf16[2048,768]{1,0:T(8,128)(2,1)}) %all-gather.7.cloned.1.call-update) | async-done | bytes 3145744 | tf_op jit(solution)/shard_map/all_gather | solution.py:142
  213.8 18.4 %multiply_convert_fusion.1 = (bf16[2048,768]{1,0:T(8,128)(2,1)S(1)}, f32[2048,768]{1,0:T(8,128)}, f32[2048,768]{1,0:T(8,128)}) fusion(f32[768]{0:T(1024)S(1)} %convert_element_type.146, bf16[2048,768]{1,0:T(8,128)(2,1)} %all-gather.7.cloned.1.call-done, bf16[768,768]{1,0:T(8,128)(2,1)S(1)} %copy-done), kind=kOutput, calls=%fused_computation.75 | convolution fusion | flops 2519728128 | bytes 20057088 | tf_op jit(solution)/shard_map/dot_general | solution.py:143
  233.9 4.0 fusion.92
  241.8 34.1 %reduce-scatter.7.cloned.1.call-done = bf16[512,768]{1,0:T(8,128)(2,1)} async-done(((bf16[2048,768]{1,0:T(8,128)(2,1)}), bf16[512,768]{1,0:T(8,128)(2,1)}) %reduce-scatter.7.cloned.1.call-update) | async-done | bytes 786448 | tf_op jit(solution)/shard_map/reduce_scatter | solution.py:148
  275.9 1.9 fusion.88
  283.6 28.4 %all-gather.9.cloned.1.call-done = bf16[2048,768]{1,0:T(8,128)(2,1)} async-done(((bf16[512,768]{1,0:T(8,128)(2,1)}), bf16[2048,768]{1,0:T(8,128)(2,1)}) %all-gather.9.cloned.1.call-update) | async-done | bytes 3145744 | tf_op jit(solution)/shard_map/all_gather | solution.py:159
  311.9 11.1 %convert_reduce_fusion.1 = (f32[768]{0:T(1024)}, bf16[2048,768]{1,0:T(8,128)(2,1)S(1)}) fusion(f32[2048,768]{1,0:T(8,128)} %get-tuple-element.205, f32[2048,768]{1,0:T(8,128)} %get-tuple-element.223, f32[768]{0:T(1024)S(1)} %copy-done.31, bf16[2048,768]{1,0:T(8,128)(2,1)} %all-gather.9.cloned.1.call-done, bf16[768,768]{1,0:T(8,128)(2,1)} %param.31), kind=kOutput, calls=%fused_computation.72 | convolution fusion | flops 2442657024 | bytes 20060160 | tf_op jit(solution)/shard_map/sd,fd->sf/dot_general | solution.py:166
  323.0 1.7 copy-done.42
  324.7 4.0 fusion.93
  328.8 38.0 %reduce-scatter.9.cloned.1.call-done = bf16[512,768]{1,0:T(8,128)(2,1)} async-done(((bf16[2048,768]{1,0:T(8,128)(2,1)}), bf16[512,768]{1,0:T(8,128)(2,1)}) %reduce-scatter.9.cloned.1.call-update) | async-done | bytes 786448 | tf_op jit(solution)/shard_map/reduce_scatter | solution.py:171
  366.8 2.7 multiply_reduce_fusion.1
  369.5 2.4 fusion.86
  374.7 6.8 convolution_convert_fusion.1
  381.5 3.8 convolution_convert_fusion.2
  385.3 17.5 %all-gather.11.cloned.1.call-done = bf16[2048,768]{1,0:T(8,128)(2,1)} async-done(((bf16[512,768]{1,0:T(8,128)(2,1)}), bf16[2048,768]{1,0:T(8,128)(2,1)}) %all-gather.11.cloned.1.call-update) | async-done | bytes 3145744 | tf_op jit(solution)/shard_map/all_gather | solution.py:178
  402.8 3.1 convolution_convert_fusion
  406.9 75.3 %while.29 = (s32[]{:T(128)}, bf16[6,1024,64]{1,2,0:T(8,128)(2,1)S(1)}, bf16[6,1024,64]{1,2,0:T(8,128)(2,1)}, bf16[6,1024,64]{1,2,0:T(8,128)(2,1)}, s32[6,1024]{1...) while((s32[]{:T(128)}, ...), condition=%wide.region_17.18_spmd, body=%wide.region_15.17_spmd.sunk | while | flops 683801600 | bytes 34141316 | solution.py:189
  410.2 2.8 multiply_reduce_fusion.6
  414.2 2.4 fusion.146
  422.7 2.8 multiply_reduce_fusion.6
  426.7 2.4 fusion.146
  435.2 2.8 multiply_reduce_fusion.6
  439.2 2.4 fusion.146
  447.8 2.8 multiply_reduce_fusion.6
  451.8 2.4 fusion.146
  460.3 2.8 multiply_reduce_fusion.6
  464.3 2.4 fusion.146
  472.8 2.8 multiply_reduce_fusion.6
  476.8 2.4 fusion.146
  484.1 2.9 fusion.80
  489.4 2.9 fusion.74
  493.4 5.2 convolution_bitcast_fusion.1
  499.9 2.4 convert_reduce_fusion
  502.4 11.7 %all-reduce = f32[4,4,768]{2,1,0:T(4,128)S(1)} all-reduce(f32[4,4,768]{2,1,0:T(4,128)S(1)} %broadcast_in_dim.105), channel_id=6, replica_groups=mesh['dp'=8,'tensor'=4] {'tensor'}, use_global_device_ids=true, to_apply=%region_30.31.clone | all-reduce | flops 12288 | bytes 98304
  515.2 2.4 convert_reduce_fusion.2
  517.6 39.2 %all-reduce.1 = (f32[2,192]{1,0:T(2,128)}, f32[768]{0:T(1024)}, f32[4,768]{1,0:T(4,128)S(1)}, f32[768]{0:T(1024)}, f32[768]{0:T(1024)}) all-reduce(f32[2,192]{1,0:T(2,128)S(1)} %pad_maximum_fusion.4, f32[768]{0:T(1024)S(1)} %convert_reduce_fusion.2, ...), channel_id=1, replica_groups=mesh['dp'=8,'tensor'=4] {'dp'}, use_global_device_ids=true, to_apply=%region_22.23 | all-reduce | flops 5760 | bytes 46080 | tf_op jit(solution)/shard_map/psum | solution.py:231
  557.4 74.4 %all-reduce.5.cloned.1.call-done = (bf16[3,768,192]{1,2,0:T(8,128)(2,1)}, bf16[192,768]{1,0:T(8,128)(2,1)}, bf16[768,768]{1,0:T(8,128)(2,1)}, bf16[768,768]{1,0:T(8,128)(2,1)}) async-done(((bf16[3,768,192]{1,2,0:T(8,128)(2,1)}, bf16[192,768]{1,0:T(8,128)(2,1)}, bf16[768,768]{1,0:T(8,128)(2,1)}, bf16[768,768]{1,0:T(8,128)(2,1)}), (bf16[3,768,192]{1,2,0:T(8,128)(2,1)}, bf16[192,768]{1,0:T(8,128)(2,1)}, ...) | async-done | bytes 3538960 | tf_op jit(solution)/shard_map/psum | solution.py:228
  631.8 3.0 convert_element_type.170
  638.6 32.7 %reduce-scatter.11.cloned.1.call-done = bf16[512,768]{1,0:T(8,128)(2,1)} async-done(((bf16[2048,768]{1,0:T(8,128)(2,1)}), bf16[512,768]{1,0:T(8,128)(2,1)}) %reduce-scatter.11.cloned.1.call-update) | async-done | bytes 786448 | tf_op jit(solution)/shard_map/reduce_scatter | solution.py:222
  671.3 2.3 add_convert_fusion.1
  (262 shorter events, 123.3 us)
Async XLA Ops:
  7.2 206.6 %copy-start = (bf16[768,768]{1,0:T(8,128)(2,1)S(1)}, bf16[768,768]{1,0:T(8,128)(2,1)}, u32[]{:S(2)}) copy-start(bf16[768,768]{1,0:T(8,128)(2,1)} %param.29) | copy-start | bytes 3538948
  7.2 33.6 %all-gather.5.cloned.1.call-start = ((), (), s32[]{:S(2)}) async-start(), calls=%async_computation.4 | async-start | bytes 3932160 | tf_op jit(solution)/shard_map/all_gather | solution.py:116
  7.9 172.7 %reduce-scatter.5.cloned.1.call-start = ((), (), s32[]{:S(2)}) async-start(), calls=%async_computation.5 | async-start | bytes 3932160 | tf_op jit(solution)/shard_map/reduce_scatter | solution.py:132
  12.3 33.5 %copy-start.28 = (pred[3]{0:T(512)(128)(4,1)}, pred[3]{0:T(512)(128)(4,1)S(1)}, u32[]{:S(2)}) copy-start(pred[3]{0:T(512)(128)(4,1)S(1)} %broadcast_compare_fusion) | copy-start | bytes 13
  54.7 1.9 copy-start.2
  67.7 1.9 copy-start.2
  80.8 1.9 copy-start.2
  93.8 1.9 copy-start.2
  106.8 1.9 copy-start.2
  119.8 1.9 copy-start.2
  130.4 8.6 %copy-start.11 = (bf16[6,1024,64]{2,1,0:T(8,128)(2,1)}, bf16[6,1024,64]{2,1,0:T(8,128)(2,1)S(1)}, u32[]{:S(2)}) copy-start(bf16[6,1024,64]{2,1,0:T(8,128)(2,1)S(1)} %get-tuple-element.470) | copy-start | bytes 2359300
  130.4 9.5 %copy-start.19 = (bf16[192,768]{1,0:T(8,128)(2,1)S(1)}, bf16[192,768]{1,0:T(8,128)(2,1)}, u32[]{:S(2)}) copy-start(bf16[192,768]{1,0:T(8,128)(2,1)} %param.25) | copy-start | bytes 884740
  138.9 0.9 copy-start.9
  142.5 0.7 copy-start.33
  142.5 0.7 copy-start.34
  142.6 0.7 copy-start.35
  142.6 38.1 %copy-start.3 = (bf16[512,768]{1,0:T(8,128)(2,1)S(1)}, bf16[512,768]{1,0:T(8,128)(2,1)}, u32[]{:S(2)}) copy-start(bf16[512,768]{1,0:T(8,128)(2,1)} %param.20) | copy-start | bytes 2359300
  142.6 71.2 %all-gather.7.cloned.1.call-start = ((), (), s32[]{:S(2)}) async-start(), calls=%async_computation.6 | async-start | bytes 3932160 | tf_op jit(solution)/shard_map/all_gather | solution.py:142
  143.3 41.9 %copy-start.22 = (f32[768]{0:T(1024)}, f32[768]{0:T(1024)S(1)}, u32[]{:S(2)}) copy-start(f32[768]{0:T(1024)S(1)} %convert_element_type.144) | copy-start | bytes 9220
  143.3 42.1 %copy-start.36 = (bf16[768]{0:T(1024)(128)(2,1)S(1)}, bf16[768]{0:T(1024)(128)(2,1)}, u32[]{:S(2)}) copy-start(bf16[768]{0:T(1024)(128)(2,1)} %param.30) | copy-start | bytes 4612
  180.6 3.1 copy-start.4
  183.7 48.5 %copy-start.23 = (f32[512]{0:T(512)}, f32[512]{0:T(512)S(1)}, u32[]{:S(2)}) copy-start(f32[512]{0:T(512)S(1)} %multiply_reduce_fusion.4) | copy-start | bytes 6148
  185.1 90.8 %reduce-scatter.7.cloned.1.call-start = ((), (), s32[]{:S(2)}) async-start(), calls=%async_computation.7 | async-start | bytes 3932160 | tf_op jit(solution)/shard_map/reduce_scatter | solution.py:148
  185.4 46.8 %copy-start.30 = (f32[768]{0:T(1024)}, f32[768]{0:T(1024)S(1)}, u32[]{:S(2)}) copy-start(f32[768]{0:T(1024)S(1)} %convert_element_type.146) | copy-start | bytes 9220
  213.8 20.1 %copy-start.39 = (bf16[768,768]{1,0:T(8,128)(2,1)S(1)}, bf16[768,768]{1,0:T(8,128)(2,1)}, u32[]{:S(2)}) copy-start(bf16[768,768]{1,0:T(8,128)(2,1)} %param.31) | copy-start | bytes 3538948
  232.2 1.7 copy-start.41
  237.9 40.3 %copy-start.12 = (bf16[512,768]{1,0:T(8,128)(2,1)S(1)}, bf16[512,768]{1,0:T(8,128)(2,1)}, u32[]{:S(2)}) copy-start(bf16[512,768]{1,0:T(8,128)(2,1)} %param.35) | copy-start | bytes 2359300
  237.9 74.0 %all-gather.9.cloned.1.call-start = ((), (), s32[]{:S(2)}) async-start(), calls=%async_computation.8 | async-start | bytes 3932160 | tf_op jit(solution)/shard_map/all_gather | solution.py:159
  275.9 2.2 copy-start.21
  275.9 3.5 copy-start.27
  281.0 1.2 copy-start.5
  281.0 30.9 %copy-start.31 = (f32[768]{0:T(1024)S(1)}, f32[768]{0:T(1024)}, u32[]{:S(2)}) copy-start(f32[768]{0:T(1024)} %copy-done.30) | copy-start | bytes 9220
  283.3 83.5 %reduce-scatter.9.cloned.1.call-start = ((), (), s32[]{:S(2)}) async-start(), calls=%async_computation.9 | async-start | bytes 3932160 | tf_op jit(solution)/shard_map/reduce_scatter | solution.py:171
  323.0 1.7 copy-start.42
  328.7 40.8 %copy-start.24 = (f32[512]{0:T(512)S(1)}, f32[512]{0:T(512)}, u32[]{:S(2)}) copy-start(f32[512]{0:T(512)} %copy-done.23) | copy-start | bytes 6148
  328.8 74.0 %all-gather.11.cloned.1.call-start = ((), (), s32[]{:S(2)}) async-start(), calls=%async_computation.10 | async-start | bytes 3932160 | tf_op jit(solution)/shard_map/all_gather | solution.py:178
  366.8 2.7 copy-start.13
  371.9 1.1 copy-start.6
  374.1 257.7 %all-reduce.5.cloned.1.call-start = ((), (), s32[]{:S(2)}) async-start(), calls=%async_computation.12 | async-start | bytes 7077888 | tf_op jit(solution)/shard_map/psum | solution.py:228
  374.7 6.8 %copy-start.38 = (bf16[2048,768]{1,0:T(8,128)(2,1)S(1)}, bf16[2048,768]{1,0:T(8,128)(2,1)}, u32[]{:S(2)}) copy-start(bf16[2048,768]{1,0:T(8,128)(2,1)} %all-gather.7.cloned.1.call-done) | copy-start | bytes 9437188
  374.7 6.8 copy-start.43
  381.5 21.3 %copy-start.20 = (bf16[192,768]{1,0:T(8,128)(2,1)S(1)}, bf16[192,768]{1,0:T(8,128)(2,1)}, u32[]{:S(2)}) copy-start(bf16[192,768]{1,0:T(8,128)(2,1)} %param.25) | copy-start | bytes 884740
  482.1 1.9 copy-start.29
  484.1 3.1 copy-start.8
  484.1 3.1 copy-start.10
  487.1 1.7 copy-start.16
  487.1 2.3 copy-start.37
  492.3 1.1 copy-start.17
  492.3 179.0 %reduce-scatter.11.cloned.1.call-start = ((), (), s32[]{:S(2)}) async-start(), calls=%async_computation.11 | async-start | bytes 3932160 | tf_op jit(solution)/shard_map/reduce_scatter | solution.py:222
  498.7 0.7 copy-start.40
  498.7 1.2 copy-start.26
  498.7 1.2 copy-start.25
  502.3 15.3 %copy-start.32 = (f32[768]{0:T(1024)S(1)}, f32[768]{0:T(1024)}, u32[]{:S(2)}) copy-start(f32[768]{0:T(1024)} %get-tuple-element.196) | copy-start | bytes 9220
  631.8 3.0 copy-start.14
  631.8 4.6 copy-start.15
  634.8 2.9 copy-start.18
  634.8 36.5 %copy-start.7 = (f32[512,768]{1,0:T(8,128)S(1)}, f32[512,768]{1,0:T(8,128)}, u32[]{:S(2)}) copy-start(f32[512,768]{1,0:T(8,128)} %copy-done.6) | copy-start | bytes 4718596
  636.4 37.2 %copy-start.1 = (bf16[768,768]{1,0:T(8,128)(2,1)S(1)}, bf16[768,768]{1,0:T(8,128)(2,1)}, u32[]{:S(2)}) copy-start(bf16[768,768]{1,0:T(8,128)(2,1)} %param.29) | copy-start | bytes 3538948
Sparse Core Ops, SparseCore 0:
  9.6 31.2 all-gather.4
  142.7 37.8 reduce-scatter.4
  185.2 28.4 all-gather.6
  238.0 37.8 reduce-scatter.6
  283.4 28.4 all-gather.8
  328.9 37.8 reduce-scatter.8
  374.3 28.4 all-gather.10
  492.5 139.3 all-reduce.4
  634.3 36.8 reduce-scatter.10
